TPU v7x, 256 devices: a whole 4x4x8 slice. The times are simulated.
256 devices in a mesh: dp: 4 (over y), space: 64 (over x, z, core).
Axes of the slice: x: 4, y: 4, z: 8, core: 2. Of those that a mesh axis runs over, the one named last changes fastest.
Arguments:
- volume: bfloat16 [4, 128, 4, 64, 128], P('dp', 'space'), may hold values from -30 to 30
- weights_one: bfloat16 [3, 3, 3, 128, 256], replicated, may hold values from -0.109375 to 0.109375
- gain_one: float32 [256], replicated, may hold values from 0.1 to 1.9
- shift_one: float32 [256], replicated, may hold values from -3 to 3
- weights_two: bfloat16 [3, 3, 3, 8, 256], P(None, None, None, None, 'space'), may hold values from -0.4375 to 0.4375
- gain_two: float32 [256], P('space'), may hold values from 0.1 to 1.9
- shift_two: float32 [256], P('space'), may hold values from -3 to 3
- upstream: bfloat16 [4, 256, 64, 2, 32], P('dp', 'space'), may hold values from -6 to 6
Outputs:
- result: bfloat16 [4, 256, 64, 2, 32], P('dp', 'space')
- grad_weights_one: float32 [3, 3, 3, 128, 256], P(None, None, None, None, 'space')
- grad_weights_two: float32 [3, 3, 3, 8, 256], P(None, None, None, None, 'space')
All inputs are finite; a program needn't handle non-finite values.
Results may differ from a plain program's by a relative error of at most 0.0057.
Values may be sent and summed in bfloat16 or wider, within the bound.
A program may use at most 64 MiB of HBM per device.

v0:
```python
import math
import jax
import jax.numpy as jnp
from jax import lax
from jax.sharding import PartitionSpec as P

EPS = 1e-05
LAST = ("NDHWC", "DHWIO", "NDHWC")
FIRST = ("NCDHW", "DHWIO", "NCDHW")


def from_behind(value, axis, steps):
    count = lax.axis_size(axis)
    leading, last = (max(0, -steps), min(count, count - steps))
    return lax.ppermute(value, axis, [(source, source + steps) for source in range(leading, last)])


def combined_all(part, axis, combine):
    gathered = jax.tree.map(lambda a: lax.all_gather(a, axis), part)

    def take(source):
        return jax.tree.map(lambda a: lax.dynamic_index_in_dim(a, source, 0, False), gathered)

    return lax.fori_loop(
        1, lax.axis_size(axis), lambda source, state: combine(state, take(source)), take(0)
    )


def welford(left, right):
    count_a, mean_a, spread_a = left
    count_b, mean_b, spread_b = right
    merged = count_a + count_b
    delta = mean_b - mean_a
    return (
        merged,
        mean_a + delta * (count_b / merged),
        spread_a + spread_b + delta * delta * (count_a * count_b / merged),
    )


def group_filter(inputs, grads):
    return lax.conv_general_dilated(
        inputs,
        grads,
        (1, 1, 1),
        ((1, 1), (1, 1), (1, 1)),
        dimension_numbers=("CNDHW", "IODHW", "DHWNC"),
        preferred_element_type=jnp.float32,
    )


def per_device(
    volume, weights_one, gain_one, shift_one, weights_two, gain_two, shift_two, upstream
):
    planes = lax.axis_size("space")
    below = from_behind(volume[:, 1:], "space", 1)
    stacked = jnp.concatenate([below, volume], axis=1)
    pre_one = lax.conv_general_dilated(
        stacked,
        weights_one,
        (2, 2, 2),
        ((0, 0), (1, 1), (1, 1)),
        dimension_numbers=LAST,
        preferred_element_type=jnp.float32,
    )
    lead = pre_one.shape[0]
    count = float(lax.axis_size("dp") * lead * planes * pre_one.shape[2] * pre_one.shape[3])
    axes_last = (0, 1, 2, 3)
    mean_one = lax.psum(jnp.sum(pre_one, axis=axes_last), ("dp", "space")) / count
    spread_one = lax.psum(jnp.sum(jnp.square(pre_one - mean_one), axis=axes_last), ("dp", "space"))
    var_one = spread_one / count
    inv_one = lax.rsqrt(var_one + EPS)
    norm_one = (pre_one - mean_one) * inv_one
    act_in = norm_one * gain_one + shift_one
    activated = jax.nn.silu(act_in).astype(jnp.bfloat16)
    act_first = jnp.transpose(activated, (0, 4, 1, 2, 3))
    own_width = weights_two.shape[4]
    group_width = weights_two.shape[3]
    window = max(own_width, group_width)
    replicas = window // own_width
    channels = act_first.shape[1]
    tail = act_first.shape[2:]
    parts = act_first.reshape((lead, channels // window, 1, window) + tail)
    copies = jnp.broadcast_to(parts, (lead, channels // window, replicas, window) + tail)
    outgoing = copies.reshape((lead, planes * window) + tail)
    inputs = lax.all_to_all(outgoing, "space", split_axis=1, concat_axis=2, tiled=True)
    groups_here = window // group_width
    per_group = own_width // groups_here
    padding_one = ((1, 1), (1, 1), (1, 1))
    pre_two = lax.conv_general_dilated(
        inputs,
        weights_two,
        (1, 1, 1),
        padding_one,
        dimension_numbers=FIRST,
        feature_group_count=groups_here,
        preferred_element_type=jnp.float32,
    )
    axes_first = (0, 2, 3, 4)
    local_mean_two = jnp.mean(pre_two, axis=axes_first, keepdims=True)
    local_spread_two = jnp.sum(jnp.square(pre_two - local_mean_two), axis=axes_first, keepdims=True)
    local_count_two = float(pre_two.size // pre_two.shape[1])
    merged_two, mean_two, spread_two = combined_all(
        (jnp.full((1, 1, 1, 1, 1), local_count_two, jnp.float32), local_mean_two, local_spread_two),
        "dp",
        welford,
    )
    inv_two = lax.rsqrt(spread_two / merged_two + EPS)
    norm_two = (pre_two - mean_two) * inv_two
    gain_col = gain_two.reshape((1, -1, 1, 1, 1))
    shift_col = shift_two.reshape((1, -1, 1, 1, 1))
    result = (norm_two * gain_col + shift_col).astype(jnp.bfloat16)
    grad_norm_two = upstream.astype(jnp.float32) * gain_col * (1.0 / math.sqrt(count))
    first_sum, second_sum = lax.psum(
        (
            jnp.sum(grad_norm_two, axis=axes_first, keepdims=True),
            jnp.sum(grad_norm_two * norm_two, axis=axes_first, keepdims=True),
        ),
        "dp",
    )
    grad_pre_two = (
        inv_two * (grad_norm_two - first_sum / count - norm_two * (second_sum / count))
    ).astype(jnp.bfloat16)
    grouped_inputs = inputs.reshape((lead, groups_here, group_width) + inputs.shape[2:])
    grouped_grads = grad_pre_two.reshape((lead, groups_here, per_group) + grad_pre_two.shape[2:])
    pieces = jax.vmap(group_filter, in_axes=(1, 1))(grouped_inputs, grouped_grads)
    local_two = jnp.transpose(pieces, (1, 2, 3, 4, 0, 5)).reshape((3, 3, 3, group_width, own_width))
    grad_weights_two = lax.psum(local_two, "dp")
    flipped = weights_two[::-1, ::-1, ::-1]
    turned = (
        flipped.reshape((3, 3, 3, group_width, groups_here, per_group))
        .transpose((0, 1, 2, 5, 4, 3))
        .reshape((3, 3, 3, per_group, window))
    )
    partial_grad = lax.conv_general_dilated(
        grad_pre_two,
        turned,
        (1, 1, 1),
        padding_one,
        dimension_numbers=FIRST,
        feature_group_count=groups_here,
        preferred_element_type=jnp.float32,
    )
    arrived = lax.all_to_all(partial_grad, "space", split_axis=2, concat_axis=1, tiled=True)
    grad_act = jnp.sum(
        arrived.reshape((lead, channels // window, replicas, window) + arrived.shape[2:]), axis=2
    ).reshape((lead, channels) + arrived.shape[2:])
    grad_last = jnp.transpose(grad_act, (0, 2, 3, 4, 1))
    sigma = jax.nn.sigmoid(act_in)
    grad_norm_one = grad_last * (sigma * (1.0 + act_in * (1.0 - sigma))) * gain_one
    third_sum, fourth_sum = lax.psum(
        (jnp.sum(grad_norm_one, axis=axes_last), jnp.sum(grad_norm_one * norm_one, axis=axes_last)),
        ("dp", "space"),
    )
    grad_pre_one = (
        inv_one * (grad_norm_one - third_sum / count - norm_one * (fourth_sum / count))
    ).astype(jnp.bfloat16)
    local_one = lax.conv_general_dilated(
        stacked,
        grad_pre_one,
        (1, 1, 1),
        ((0, 0), (1, 0), (1, 0)),
        rhs_dilation=(2, 2, 2),
        dimension_numbers=("CDHWN", "IDHWO", "DHWNC"),
        preferred_element_type=jnp.float32,
    )
    summed = lax.psum(local_one, "dp")
    grad_weights_one = lax.psum_scatter(summed, "space", scatter_dimension=4, tiled=True)
    return (result, grad_weights_one, grad_weights_two)


def solution(mesh):
    return jax.shard_map(
        per_device,
        mesh=mesh,
        in_specs=(
            P("dp", "space", None, None, None),
            P(),
            P(),
            P(),
            P(None, None, None, None, "space"),
            P("space"),
            P("space"),
            P("dp", "space", None, None, None),
        ),
        out_specs=(
            P("dp", "space", None, None, None),
            P(None, None, None, None, "space"),
            P(None, None, None, None, "space"),
        ),
        check_vma=False,
    )
```

profile of v0, /device:TPU:2, one launch (start us, length us, event | category | flops | bytes accessed | tf_op | source)
XLA Modules:
  0.0 559.2 jit_solution(1003987523249396105)
XLA Ops:
  7.2 1.0 slice.21
  8.3 1.9 collective-permute-start
  10.2 7.9 %collective-permute-done = bf16[1,1,4,64,128]{4,0,3,2,1:T(2,128)(2,1)S(1)} collective-permute-done((bf16[1,1,4,64,128]{4,0,3,2,1:T(2,128)(2,1)S(1)}, bf16[1,1,4,64,128]{4,0,3,2,1:T(2,128)(2,1)S(1)}, u32[]{:S(2)}, u32[]{:S(2)}) %collective-permute-start) | collective-permute-done | bytes 65568 | tf_op jit(solution)/shard_map/ppermute | solution.py:15
  18.1 0.1 constant_dynamic-update-slice_fusion.1
  18.2 1.1 constant_dynamic-update-slice_fusion
  19.4 0.7 copy-done.1
  20.2 0.2 copy.244
  20.5 0.4 select_reduce_fusion.3
  21.0 74.9 %psum.56 = f32[256]{0:T(256)S(1)} all-reduce(f32[256]{0:T(256)S(1)} %get-tuple-element.289), channel_id=1, replica_groups=mesh['dp'=4,'space'=64] {'dp','space'}, use_global_device_ids=true, to_apply=%region_1.0 | all-reduce | flops 256 | bytes 2048 | tf_op jit(solution)/shard_map/psum | solution.py:69
  95.9 74.4 %psum.57 = f32[256]{0:T(256)S(1)} all-reduce(f32[256]{0:T(256)S(1)} %select_reduce_fusion.2), channel_id=1, replica_groups=mesh['dp'=4,'space'=64] {'dp','space'}, use_global_device_ids=true, to_apply=%region_3.0 | all-reduce | flops 256 | bytes 2048 | tf_op jit(solution)/shard_map/psum | solution.py:70
  170.5 0.4 copy-done.9
  171.1 0.1 copy.203
  171.2 0.1 broadcast_in_dim.11
  171.3 0.8 reshape.180
  172.2 8.1 %all-to-all-start = ((bf16[64,2,256]{2,1,0:T(2,128)(2,1)}), bf16[64,2,256]{2,1,0:T(2,128)(2,1)S(1)}, u32[]{:S(2)}, u32[]{:S(2)}) async-start(bf16[64,2,256]{2,1,0:T(2,128)(2,1)} %reshape.180), calls=%async_computation | async-start | bytes 131072 | tf_op jit(solution)/shard_map/all_to_all | solution.py:86
  180.3 0.6 rev.3
  180.9 0.6 dynamic-slice
  182.2 0.8 dynamic-update-slice
  183.0 6.0 %all-to-all-done = bf16[64,2,256]{2,1,0:T(2,128)(2,1)S(1)} async-done(((bf16[64,2,256]{2,1,0:T(2,128)(2,1)}), bf16[64,2,256]{2,1,0:T(2,128)(2,1)S(1)}, u32[]{:S(2)}, u32[]{:S(2)}) %all-to-all-start) | async-done | bytes 65568 | tf_op jit(solution)/shard_map/all_to_all | solution.py:86
  189.1 0.2 reshape.181
  189.3 0.2 copy.245
  189.5 0.7 pad.2.clone
  190.2 2.1 copy.207
  192.3 0.2 slice.24
  192.5 5.6 fusion.8
  198.1 1.7 copy.208
  199.8 0.2 select_reduce_fusion.1
  200.1 0.2 select_reduce_fusion
  200.3 0.2 dynamic-update-slice.2
  200.5 8.6 %all-reduce.7 = (f32[4]{0:T(128)S(1)}, f32[16]{0:T(128)S(1)}, f32[16]{0:T(128)S(1)}) all-reduce(f32[4]{0:T(128)S(1)} %dynamic-update-slice, f32[16]{0:T(128)S(1)} %get-tuple-element.288, f32[16]{0:T(128)S(1)} %dynamic-update-slice.2), channel_id=1, replica_groups=mesh['dp'=4,'space'=64] {'dp'}, use_global_device_ids=true, to_apply=%add | all-reduce | flops 36 | bytes 288
  209.8 13.6 %while.19 = (s32[]{:T(128)}, f32[1,1,1,1,1]{4,3,2,1,0:T(1,128)}, f32[1,4,1,1,1]{1,4,3,2,0:T(1,128)S(1)}, f32[1,4,1,1,1]{1,4,3,2,0:T(1,128)S(1)}, f32[4,1,1,1,1,1...) while((s32[]{:T(128)}, f32[1,1,1,1,1]{4,3,2,1,0:T(1,128)}, ...), condition=%wide.region_7.8_spmd, body=%wide.region_6.7_spmd.sunk | while | flops 37 | bytes 303 | solution.py:24
  209.8 0.6 constant_dynamic-slice_fusion.5
  214.4 0.6 constant_dynamic-slice_fusion.5
  218.9 0.6 constant_dynamic-slice_fusion.5
  223.5 0.7 rsqrt_bitcast_fusion
  224.1 0.8 add_convert_fusion
  224.9 0.3 fusion.39
  225.2 9.4 %all-reduce.6 = (f32[1,4,1,1,1]{1,4,3,2,0:T(1,128)S(1)}, f32[1,4,1,1,1]{1,4,3,2,0:T(1,128)S(1)}) all-reduce(f32[1,4,1,1,1]{1,4,3,2,0:T(1,128)S(1)} %bitcast.177, f32[1,4,1,1,1]{1,4,3,2,0:T(1,128)S(1)} %bitcast.176), channel_id=1, replica_groups=mesh['dp'=4,'space'=64] {'dp'}, use_global_device_ids=true, to_apply=%region_11.12 | all-reduce | flops 8 | bytes 64 | tf_op jit(solution)/shard_map/psum | solution.py:114
  234.9 0.4 copy.218
  235.3 0.2 slice.28
  235.5 6.9 %convolution_select_fusion = f32[64,2,8,5,8]{4,2,3,1,0:T(8,128)} fusion(pred[8,5]{0,1:T(8,128)(4,1)S(1)} %copy-done.7, bf16[4,64,2,1,7,2]{4,0,5,2,1,3:T(4,128)(2,1)S(1)} %slice.28, bf16[4,64,2,1,8,5]{4,0,5,2,1,3:T(4,128)(2,1)S(1)} %copy.218, bf16[3,3,3,8,4]{3,4,2,1,0:T(4,128)(2,1)S(1)} %copy-done.6), kind=kOutput, calls=%fused_computation.19 | convolution fusion | flops 6049792 | bytes 220904 | tf_op jit(solution)/shard_map/conv_general_dilated | solution.py:135
  242.5 2.6 copy.219
  245.1 0.3 copy.220
  245.4 0.9 reshape.182
  246.4 5.5 all-to-all-start.1
  252.2 0.8 copy.241
  253.0 8.2 %all-to-all-done.1 = f32[64,1,512]{2,1,0:T(1,128)S(1)} async-done(((f32[64,1,512]{2,1,0:T(1,128)}), f32[64,1,512]{2,1,0:T(1,128)S(1)}, u32[]{:S(2)}, u32[]{:S(2)}) %all-to-all-start.1) | async-done | bytes 131104 | tf_op jit(solution)/shard_map/all_to_all | solution.py:144
  261.2 0.5 broadcast.186
  261.7 0.9 reduce.1
  262.7 0.2 reshape.183
  262.9 0.7 reduce_sum.87
  263.6 1.3 fusion.51
  264.9 73.3 %all-reduce.4 = (f32[256]{0:T(256)S(1)}, f32[256]{0:T(256)S(1)}) all-reduce(f32[256]{0:T(256)S(1)} %get-tuple-element.252, f32[256]{0:T(256)S(1)} %get-tuple-element.251), channel_id=1, replica_groups=mesh['dp'=4,'space'=64] {'dp','space'}, use_global_device_ids=true, to_apply=%region_16.17 | all-reduce | flops 512 | bytes 4096 | tf_op jit(solution)/shard_map/psum | solution.py:151
  338.4 0.8 fusion.31
  339.4 2.8 fusion.53
  342.3 0.6 copy-done.13
  342.9 0.6 dynamic-slice.3
  344.1 3.5 copy.231
  347.7 0.6 copy.232
  348.3 3.4 copy.230
  351.7 29.6 %fusion.54 = f32[3,3,3,8,4]{3,4,2,1,0:T(4,128)S(1)} fusion(bf16[1,8,64,2,32]{1,0,4,3,2:T(2,128)(2,1)} %copy.230, bf16[1,4,64,2,32]{1,0,4,3,2:T(2,128)(2,1)} %copy.231), kind=kOutput, calls=%fused_computation.97 | convolution fusion | flops 4572160 | bytes 101760 | tf_op jit(solution)/shard_map/vmap()/conv_general_dilated | solution.py:42
  381.3 151.0 %all-reduce.10.cloned.1.call-done = f32[3,3,3,128,256]{3,4,2,1,0:T(8,128)} async-done(((f32[3,3,3,128,256]{3,4,2,1,0:T(8,128)}), f32[3,3,3,128,256]{3,4,2,1,0:T(8,128)}) %all-reduce.10.cloned.1.call-update) | async-done | bytes 3538960
  532.3 0.9 constant_dynamic-slice_fusion.3
  533.3 18.7 %all-reduce.5 = (f32[3,3,3,128,4]{3,4,2,1,0:T(4,128)}, f32[3,3,3,8,4]{3,4,2,1,0:T(4,128)}) all-reduce(f32[3,3,3,128,4]{3,4,2,1,0:T(4,128)S(1)} %constant_dynamic-slice_fusion.3, f32[3,3,3,8,4]{3,4,2,1,0:T(4,128)S(1)} %fusion.54), channel_id=1, replica_groups=mesh['dp'=4,'space'=64] {'dp'}, use_global_device_ids=true, to_apply=%region_17.18 | all-reduce | flops 14688 | bytes 117504 | tf_op jit(solution)/shard_map/psum | solution.py:167
  (75 shorter events, 2.1 us)
Async XLA Ops:
  7.2 13.3 %copy-start = (bf16[3,3,3,128,256]{4,3,2,1,0:T(8,128)(2,1)S(1)}, bf16[3,3,3,128,256]{4,3,2,1,0:T(8,128)(2,1)}, u32[]{:S(2)}) copy-start(bf16[3,3,3,128,256]{4,3,2,1,0:T(8,128)(2,1)} %param.11) | copy-start | bytes 5308420
  7.2 13.3 %copy-start.7 = (pred[8,5]{0,1:T(8,128)(4,1)S(1)}, pred[8,5]{0,1:T(8,128)(4,1)}, u32[]{:S(2)}) copy-start(pred[8,5]{0,1:T(8,128)(4,1)} %constant.99) | copy-start | bytes 124
  8.3 9.8 %collective-permute-start = (bf16[1,1,4,64,128]{4,0,3,2,1:T(2,128)(2,1)S(1)}, bf16[1,1,4,64,128]{4,0,3,2,1:T(2,128)(2,1)S(1)}, u32[]{:S(2)}, u32[]{:S(2)}) collective-permute-start(bf16[1,1,4,64,128]{4,0,3,2,1:T(2,128)(2,1)S(1)} %copy.254), channel_id=1, source_target_pairs={{0,1},{1,2},{2,3},{3,4},{4,5},{5,6},{6,7},{7,8},{8,9},{9,10},{10,1... | collective-permute-start | bytes 196616 | tf_op jit(solution)/shard_map/ppermute | solution.py:15
  19.4 0.7 copy-start.1
  20.1 150.2 %copy-start.8 = (f32[256]{0:T(256)S(1)}, f32[256]{0:T(256)}, u32[]{:S(2)}) copy-start(f32[256]{0:T(256)} %param.12) | copy-start | bytes 3076
  20.1 150.2 %copy-start.11 = (f32[256]{0:T(256)S(1)}, f32[256]{0:T(256)}, u32[]{:S(2)}) copy-start(f32[256]{0:T(256)} %param.13) | copy-start | bytes 3076
  20.5 159.8 %copy-start.5 = (bf16[3,3,3,8,4]{3,4,2,1,0:T(4,128)(2,1)S(1)}, bf16[3,3,3,8,4]{3,4,2,1,0:T(4,128)(2,1)}, u32[]{:S(2)}) copy-start(bf16[3,3,3,8,4]{3,4,2,1,0:T(4,128)(2,1)} %param.14) | copy-start | bytes 5188
  20.5 160.4 %copy-start.14 = (u32[256]{0:T(256)S(1)}, u32[256]{0:T(256)}, u32[]{:S(2)}) copy-start(u32[256]{0:T(256)} %constant.108) | copy-start | bytes 3076
  170.3 0.6 copy-start.9
  172.2 16.9 %all-to-all-start = ((bf16[64,2,256]{2,1,0:T(2,128)(2,1)}), bf16[64,2,256]{2,1,0:T(2,128)(2,1)S(1)}, u32[]{:S(2)}, u32[]{:S(2)}) async-start(bf16[64,2,256]{2,1,0:T(2,128)(2,1)} %reshape.180), calls=%async_computation | async-start | bytes 131072 | tf_op jit(solution)/shard_map/all_to_all | solution.py:86
  198.1 26.0 %copy-start.10 = (f32[4]{0:T(128)S(1)}, f32[4]{0:T(128)}, u32[]{:S(2)}) copy-start(f32[4]{0:T(128)} %param.15) | copy-start | bytes 52
  198.1 26.1 %copy-start.12 = (f32[4]{0:T(128)S(1)}, f32[4]{0:T(128)}, u32[]{:S(2)}) copy-start(f32[4]{0:T(128)} %param.16) | copy-start | bytes 52
  198.1 26.9 %copy-start.4 = (bf16[1,4,64,2,32]{2,4,3,1,0:T(8,128)(2,1)S(1)}, bf16[1,4,64,2,32]{2,4,3,1,0:T(8,128)(2,1)}, u32[]{:S(2)}) copy-start(bf16[1,4,64,2,32]{2,4,3,1,0:T(8,128)(2,1)} %param.17) | copy-start | bytes 98308
  199.8 35.7 %copy-start.6 = (bf16[3,3,3,8,4]{3,4,2,1,0:T(4,128)(2,1)S(1)}, bf16[3,3,3,8,4]{3,4,2,1,0:T(4,128)(2,1)}, u32[]{:S(2)}) copy-start(bf16[3,3,3,8,4]{3,4,2,1,0:T(4,128)(2,1)} %rev.3) | copy-start | bytes 5188
  246.4 14.9 %all-to-all-start.1 = ((f32[64,1,512]{2,1,0:T(1,128)}), f32[64,1,512]{2,1,0:T(1,128)S(1)}, u32[]{:S(2)}, u32[]{:S(2)}) async-start(f32[64,1,512]{2,1,0:T(1,128)} %reshape.182), calls=%async_computation.1 | async-start | bytes 262144 | tf_op jit(solution)/shard_map/all_to_all | solution.py:144
  251.8 280.5 %all-reduce.10.cloned.1.call-start = ((), (), s32[]{:S(2)}) async-start(), calls=%async_computation.2 | async-start | bytes 7077888
  262.7 76.7 %copy-start.2 = (bf16[1,3,4,64,128]{4,0,3,2,1:T(2,128)(2,1)S(1)}, bf16[1,3,4,64,128]{4,0,3,2,1:T(2,128)(2,1)}, u32[]{:S(2)}) copy-start(bf16[1,3,4,64,128]{4,0,3,2,1:T(2,128)(2,1)} %copy-done.1) | copy-start | bytes 589828
  342.2 0.7 copy-start.13
  342.2 5.4 copy-start.3
Sparse Core Ops, SparseCore 0:
  342.4 189.9 all-reduce.9
where the time goes:
time: 568 us; the launch traced here: 559 us
  blocking collectives  259 us (46%)
  waiting for transfers between devices  173 us (30%)
  matrix products  45.4 us (8%)
  local copies, waits for them, and re-layouts  31 us (5%)
  between operations  16.8 us (3%)
  starting transfers between devices  15.5 us (3%)
  loops' own time  11.6 us (2%)
  other arithmetic  6.47 us (1%)
    unnamed x2, waiting for transfers between devices  151 us
    psum x1, blocking collectives, per_device(): lax.psum(jnp.sum(pre_one, axis=axes_last), ('dp', 'space')) / count  74.9 us
    psum x1, blocking collectives, per_device(): lax.psum(jnp.sum(jnp.square(pre_one - mean_one), axis=axes_last), ('dp',...  74.4 us
    psum x1, blocking collectives, per_device(): lax.psum((jnp.sum(grad_norm_one, axis=axes_last), jnp.sum(grad_norm_one *...  73.3 us
    conv_general_dilated x1, matrix products, group_filter(): lax.conv_general_dilated(inputs, grads, (1, 1, 1), ((1, 1), (1, 1), (1, 1...  29.6 us
    psum x1, blocking collectives, per_device(): summed = lax.psum(local_one, 'dp')  18.7 us
    another operation x1, loops' own time, combined_all(): lax.fori_loop(1, lax.axis_size(axis), lambda source, state: combine(state...  11.6 us
  transfers between devices with their start and end apart: 4, of which 4 were waited for; matrix products, arithmetic and copies ran while one was open for 7% of the time, Pallas kernels for 0%

commit v1 on v0

--- a/solution.py
+++ b/solution.py
@@ -164,7 +164,9 @@
         dimension_numbers=("CDHWN", "IDHWO", "DHWNC"),
         preferred_element_type=jnp.float32,
     )
-    summed = lax.psum(local_one, "dp")
+    summed = local_one
+    for hop in (1, 2):
+        summed = summed + lax.ppermute(summed, "dp", [(dev, dev ^ hop) for dev in range(4)])
     grad_weights_one = lax.psum_scatter(summed, "space", scatter_dimension=4, tiled=True)
     return (result, grad_weights_one, grad_weights_two)
 

time: 568 us -> 727 us (1.28)
  waiting for transfers between devices: 173 us -> 317 us
  starting transfers between devices: 15.5 us -> 26.8 us
    ppermute x0 -> x2, waiting for transfers between devices: none -> 156 us  [per_device(): lax.ppermute(summed, 'dp', [(dev, dev ^ hop) for dev in range(4)])]
    unnamed x2, waiting for transfers between devices: 151 us -> 137 us
    ppermute x0 -> x2, starting transfers between devices: none -> 11.3 us  [per_device(): lax.ppermute(summed, 'dp', [(dev, dev ^ hop) for dev in range(4)])]
  transfers between devices with their start and end apart: 4 -> 6, of which waited for: 4 -> 6; matrix products, arithmetic and copies ran while one was open for 7% -> 5% of each run, Pallas kernels for 0% -> 0%
where the time goes in v1:
time: 727 us; the launch traced here: 718 us
  waiting for transfers between devices  317 us (44%)
  blocking collectives  257 us (35%)
  matrix products  44.6 us (6%)
  local copies, waits for them, and re-layouts  35.7 us (5%)
  starting transfers between devices  26.8 us (4%)
  between operations  16.8 us (2%)
  loops' own time  11.4 us (2%)
  other arithmetic  9.12 us (1%)
    ppermute x2, waiting for transfers between devices, per_device(): lax.ppermute(summed, 'dp', [(dev, dev ^ hop) for dev in range(4)])  156 us
    unnamed x2, waiting for transfers between devices  137 us
    psum x1, blocking collectives, per_device(): lax.psum(jnp.sum(pre_one, axis=axes_last), ('dp', 'space')) / count  74.9 us
    psum x1, blocking collectives, per_device(): lax.psum(jnp.sum(jnp.square(pre_one - mean_one), axis=axes_last), ('dp',...  74.4 us
    psum x1, blocking collectives, per_device(): lax.psum((jnp.sum(grad_norm_one, axis=axes_last), jnp.sum(grad_norm_one *...  73.3 us
    conv_general_dilated x1, matrix products, group_filter(): lax.conv_general_dilated(inputs, grads, (1, 1, 1), ((1, 1), (1, 1), (1, 1...  29.6 us
    psum x1, blocking collectives, per_device(): grad_weights_two = lax.psum(local_two, 'dp')  16.6 us
  transfers between devices with their start and end apart: 6, of which 6 were waited for; matrix products, arithmetic and copies ran while one was open for 5% of the time, Pallas kernels for 0%

profile of v1, /device:TPU:2, one launch (start us, length us, event | category | flops | bytes accessed | tf_op | source)
XLA Modules:
  0.0 718.2 jit_solution(3796037877745886450)
XLA Ops:
  7.2 1.0 slice.21
  8.3 1.9 collective-permute-start
  10.2 7.9 %collective-permute-done = bf16[1,1,4,64,128]{4,0,3,2,1:T(2,128)(2,1)S(1)} collective-permute-done((bf16[1,1,4,64,128]{4,0,3,2,1:T(2,128)(2,1)S(1)}, bf16[1,1,4,64,128]{4,0,3,2,1:T(2,128)(2,1)S(1)}, u32[]{:S(2)}, u32[]{:S(2)}) %collective-permute-start) | collective-permute-done | bytes 65568 | tf_op jit(solution)/shard_map/ppermute | solution.py:15
  18.2 1.1 constant_dynamic-update-slice_fusion
  19.5 0.7 copy-done.1
  20.5 0.4 select_reduce_fusion.3
  20.9 74.9 %psum.49 = f32[256]{0:T(256)S(1)} all-reduce(f32[256]{0:T(256)S(1)} %get-tuple-element.290), channel_id=1, replica_groups=mesh['dp'=4,'space'=64] {'dp','space'}, use_global_device_ids=true, to_apply=%region_1.0 | all-reduce | flops 256 | bytes 2048 | tf_op jit(solution)/shard_map/psum | solution.py:69
  95.9 74.4 %psum.50 = f32[256]{0:T(256)S(1)} all-reduce(f32[256]{0:T(256)S(1)} %select_reduce_fusion.2), channel_id=1, replica_groups=mesh['dp'=4,'space'=64] {'dp','space'}, use_global_device_ids=true, to_apply=%region_3.0 | all-reduce | flops 256 | bytes 2048 | tf_op jit(solution)/shard_map/psum | solution.py:70
  170.3 0.7 add_multiply_fusion
  171.5 0.8 reshape.178
  172.4 8.1 %all-to-all-start = ((bf16[64,2,256]{2,1,0:T(2,128)(2,1)}), bf16[64,2,256]{2,1,0:T(2,128)(2,1)S(1)}, u32[]{:S(2)}, u32[]{:S(2)}) async-start(bf16[64,2,256]{2,1,0:T(2,128)(2,1)} %reshape.178), calls=%async_computation | async-start | bytes 131072 | tf_op jit(solution)/shard_map/all_to_all | solution.py:86
  180.5 0.6 dynamic-slice
  181.8 0.8 dynamic-update-slice
  182.5 6.8 all-to-all-done
  189.3 0.2 reshape.179
  189.5 0.2 copy.254
  189.7 0.7 pad.2.clone
  190.4 2.1 copy.216
  192.5 0.2 slice.24
  192.7 5.6 fusion.8
  198.3 1.7 copy.217
  200.0 0.2 select_reduce_fusion.1
  200.3 0.2 select_reduce_fusion
  200.5 0.2 dynamic-update-slice.2
  200.7 8.6 %all-reduce.6 = (f32[4]{0:T(128)S(1)}, f32[16]{0:T(128)S(1)}, f32[16]{0:T(128)S(1)}) all-reduce(f32[4]{0:T(128)S(1)} %dynamic-update-slice, f32[16]{0:T(128)S(1)} %get-tuple-element.289, f32[16]{0:T(128)S(1)} %dynamic-update-slice.2), channel_id=1, replica_groups=mesh['dp'=4,'space'=64] {'dp'}, use_global_device_ids=true, to_apply=%add | all-reduce | flops 36 | bytes 288
  210.0 13.2 %while.19 = (s32[]{:T(128)}, f32[1,1,1,1,1]{4,3,2,1,0:T(1,128)}, f32[1,4,1,1,1]{1,4,3,2,0:T(1,128)S(1)}, f32[1,4,1,1,1]{1,4,3,2,0:T(1,128)S(1)}, f32[4,1,1,1,1,1...) while((s32[]{:T(128)}, f32[1,1,1,1,1]{4,3,2,1,0:T(1,128)}, ...), condition=%wide.region_7.8_spmd, body=%wide.region_6.7_spmd.sunk | while | flops 37 | bytes 303 | solution.py:24
  210.0 0.6 constant_dynamic-slice_fusion.5
  214.4 0.6 constant_dynamic-slice_fusion.5
  218.8 0.6 constant_dynamic-slice_fusion.5
  223.2 0.7 rsqrt_bitcast_fusion
  223.9 0.8 add_convert_fusion
  224.7 0.3 fusion.39
  225.0 9.2 %all-reduce.5 = (f32[1,4,1,1,1]{1,4,3,2,0:T(1,128)S(1)}, f32[1,4,1,1,1]{1,4,3,2,0:T(1,128)S(1)}) all-reduce(f32[1,4,1,1,1]{1,4,3,2,0:T(1,128)S(1)} %bitcast.175, f32[1,4,1,1,1]{1,4,3,2,0:T(1,128)S(1)} %bitcast.174), channel_id=1, replica_groups=mesh['dp'=4,'space'=64] {'dp'}, use_global_device_ids=true, to_apply=%region_11.12 | all-reduce | flops 8 | bytes 64 | tf_op jit(solution)/shard_map/psum | solution.py:114
  234.5 0.4 copy.227
  234.8 0.2 slice.28
  235.1 6.9 convolution_select_fusion
  242.0 2.7 copy.228
  244.7 0.3 copy.229
  245.0 0.9 reshape.180
  245.9 5.5 all-to-all-start.1
  251.9 8.9 %all-to-all-done.1 = f32[64,1,512]{2,1,0:T(1,128)S(1)} async-done(((f32[64,1,512]{2,1,0:T(1,128)}), f32[64,1,512]{2,1,0:T(1,128)S(1)}, u32[]{:S(2)}, u32[]{:S(2)}) %all-to-all-start.1) | async-done | bytes 131104 | tf_op jit(solution)/shard_map/all_to_all | solution.py:144
  260.8 0.5 broadcast.186
  261.3 0.9 reduce.1
  262.2 0.2 reshape.181
  262.4 0.7 reduce_sum.87
  263.2 1.2 fusion.51
  264.3 73.3 %all-reduce.4 = (f32[256]{0:T(256)S(1)}, f32[256]{0:T(256)S(1)}) all-reduce(f32[256]{0:T(256)S(1)} %get-tuple-element.255, f32[256]{0:T(256)S(1)} %get-tuple-element.254), channel_id=1, replica_groups=mesh['dp'=4,'space'=64] {'dp','space'}, use_global_device_ids=true, to_apply=%region_16.17 | all-reduce | flops 512 | bytes 4096 | tf_op jit(solution)/shard_map/psum | solution.py:151
  338.2 2.1 fusion.53
  340.3 78.2 %collective-permute-done.1 = f32[3,3,3,128,256]{4,3,2,1,0:T(8,128)S(1)} collective-permute-done((f32[3,3,3,128,256]{4,3,2,1,0:T(8,128)S(1)}, f32[3,3,3,128,256]{4,3,2,1,0:T(8,128)S(1)}, u32[]{:S(2)}, u32[]{:S(2)}) %collective-permute-start.1) | collective-permute-done | bytes 3538976 | tf_op jit(solution)/shard_map/ppermute | solution.py:169
  418.6 0.6 add.153
  419.2 11.2 %collective-permute-start.2 = (f32[3,3,3,128,256]{4,3,2,1,0:T(8,128)S(1)}, f32[3,3,3,128,256]{4,3,2,1,0:T(8,128)S(1)}, u32[]{:S(2)}, u32[]{:S(2)}) collective-permute-start(f32[3,3,3,128,256]{4,3,2,1,0:T(8,128)S(1)} %add.153), channel_id=1, source_target_pairs={{0,128},{64,192},{128,0},{192,64},{1,129},{65,193},{129,1},{193,65... | collective-permute-start | bytes 10616840 | tf_op jit(solution)/shard_map/ppermute | solution.py:169
  430.4 77.5 %collective-permute-done.2 = f32[3,3,3,128,256]{4,3,2,1,0:T(8,128)S(1)} collective-permute-done((f32[3,3,3,128,256]{4,3,2,1,0:T(8,128)S(1)}, f32[3,3,3,128,256]{4,3,2,1,0:T(8,128)S(1)}, u32[]{:S(2)}, u32[]{:S(2)}) %collective-permute-start.2) | collective-permute-done | bytes 3538976 | tf_op jit(solution)/shard_map/ppermute | solution.py:169
  507.8 2.2 add.154
  510.1 6.4 copy.238
  516.5 0.6 copy-done.11
  517.1 0.6 dynamic-slice.3
  518.4 3.4 copy.241
  521.9 0.6 copy.242
  522.5 3.2 copy.240
  525.7 29.6 %fusion.54 = f32[3,3,3,8,4]{3,4,2,1,0:T(4,128)S(1)} fusion(bf16[1,8,64,2,32]{1,0,4,3,2:T(2,128)(2,1)} %copy.240, bf16[1,4,64,2,32]{1,0,4,3,2:T(2,128)(2,1)} %copy.241), kind=kOutput, calls=%fused_computation.97 | convolution fusion | flops 4572160 | bytes 101760 | tf_op jit(solution)/shard_map/vmap()/conv_general_dilated | solution.py:42
  555.3 16.6 %psum.55 = f32[3,3,3,8,4]{3,4,2,1,0:T(4,128)} all-reduce(f32[3,3,3,8,4]{3,4,2,1,0:T(4,128)S(1)} %fusion.54), channel_id=1, replica_groups=mesh['dp'=4,'space'=64] {'dp'}, use_global_device_ids=true, to_apply=%region_18.19 | all-reduce | flops 864 | bytes 6912 | tf_op jit(solution)/shard_map/psum | solution.py:128
  572.0 137.4 %all-reduce.9.cloned.1.call-done = f32[3,3,3,128,256]{3,2,1,0,4:T(4,128)} async-done(((f32[3,3,3,128,256]{3,2,1,0,4:T(4,128)}), f32[3,3,3,128,256]{3,2,1,0,4:T(4,128)}) %all-reduce.9.cloned.1.call-update) | async-done | bytes 3538960
  709.4 0.9 constant_dynamic-slice_fusion.3
  710.3 0.6 copy.243
  (79 shorter events, 3.0 us)
Async XLA Ops:
  7.2 13.3 %copy-start = (bf16[3,3,3,128,256]{4,3,2,1,0:T(8,128)(2,1)S(1)}, bf16[3,3,3,128,256]{4,3,2,1,0:T(8,128)(2,1)}, u32[]{:S(2)}) copy-start(bf16[3,3,3,128,256]{4,3,2,1,0:T(8,128)(2,1)} %param.11) | copy-start | bytes 5308420
  7.2 13.3 %copy-start.6 = (pred[8,5]{0,1:T(8,128)(4,1)S(1)}, pred[8,5]{0,1:T(8,128)(4,1)}, u32[]{:S(2)}) copy-start(pred[8,5]{0,1:T(8,128)(4,1)} %constant.99) | copy-start | bytes 124
  8.3 9.8 %collective-permute-start = (bf16[1,1,4,64,128]{4,0,3,2,1:T(2,128)(2,1)S(1)}, bf16[1,1,4,64,128]{4,0,3,2,1:T(2,128)(2,1)S(1)}, u32[]{:S(2)}, u32[]{:S(2)}) collective-permute-start(bf16[1,1,4,64,128]{4,0,3,2,1:T(2,128)(2,1)S(1)} %copy.263), channel_id=1, source_target_pairs={{0,1},{1,2},{2,3},{3,4},{4,5},{5,6},{6,7},{7,8},{8,9},{9,10},{10,1... | collective-permute-start | bytes 196616 | tf_op jit(solution)/shard_map/ppermute | solution.py:15
  19.4 0.7 copy-start.1
  19.4 150.9 %copy-start.7 = (f32[256]{0:T(256)S(1)}, f32[256]{0:T(256)}, u32[]{:S(2)}) copy-start(f32[256]{0:T(256)} %param.12) | copy-start | bytes 3076
  19.4 150.9 %copy-start.9 = (f32[256]{0:T(256)S(1)}, f32[256]{0:T(256)}, u32[]{:S(2)}) copy-start(f32[256]{0:T(256)} %param.13) | copy-start | bytes 3076
  20.5 160.0 %copy-start.5 = (bf16[3,3,3,8,4]{3,4,2,1,0:T(4,128)(2,1)S(1)}, bf16[3,3,3,8,4]{3,4,2,1,0:T(4,128)(2,1)}, u32[]{:S(2)}) copy-start(bf16[3,3,3,8,4]{3,4,2,1,0:T(4,128)(2,1)} %param.14) | copy-start | bytes 5188
  20.5 160.0 %copy-start.12 = (u32[256]{0:T(256)S(1)}, u32[256]{0:T(256)}, u32[]{:S(2)}) copy-start(u32[256]{0:T(256)} %constant.108) | copy-start | bytes 3076
  172.4 16.9 %all-to-all-start = ((bf16[64,2,256]{2,1,0:T(2,128)(2,1)}), bf16[64,2,256]{2,1,0:T(2,128)(2,1)S(1)}, u32[]{:S(2)}, u32[]{:S(2)}) async-start(bf16[64,2,256]{2,1,0:T(2,128)(2,1)} %reshape.178), calls=%async_computation | async-start | bytes 131072 | tf_op jit(solution)/shard_map/all_to_all | solution.py:86
  198.3 25.6 %copy-start.8 = (f32[4]{0:T(128)S(1)}, f32[4]{0:T(128)}, u32[]{:S(2)}) copy-start(f32[4]{0:T(128)} %param.15) | copy-start | bytes 52
  198.3 25.6 %copy-start.10 = (f32[4]{0:T(128)S(1)}, f32[4]{0:T(128)}, u32[]{:S(2)}) copy-start(f32[4]{0:T(128)} %param.16) | copy-start | bytes 52
  198.3 26.4 %copy-start.4 = (bf16[1,4,64,2,32]{2,4,3,1,0:T(8,128)(2,1)S(1)}, bf16[1,4,64,2,32]{2,4,3,1,0:T(8,128)(2,1)}, u32[]{:S(2)}) copy-start(bf16[1,4,64,2,32]{2,4,3,1,0:T(8,128)(2,1)} %param.17) | copy-start | bytes 98308
  242.0 9.5 %copy-start.2 = (f32[1,2,8,5,256]{4,2,3,1,0:T(8,128)S(1)}, f32[1,2,8,5,256]{4,2,3,1,0:T(8,128)}, u32[]{:S(2)}) copy-start(f32[1,2,8,5,256]{4,2,3,1,0:T(8,128)} %get-tuple-element.280) | copy-start | bytes 245764
  245.9 14.9 %all-to-all-start.1 = ((f32[64,1,512]{2,1,0:T(1,128)}), f32[64,1,512]{2,1,0:T(1,128)S(1)}, u32[]{:S(2)}, u32[]{:S(2)}) async-start(f32[64,1,512]{2,1,0:T(1,128)} %reshape.180), calls=%async_computation.1 | async-start | bytes 262144 | tf_op jit(solution)/shard_map/all_to_all | solution.py:144
  251.4 458.0 %all-reduce.9.cloned.1.call-start = ((), (), s32[]{:S(2)}) async-start(), calls=%async_computation.2 | async-start | bytes 9437184
  340.2 78.3 %collective-permute-start.1 = (f32[3,3,3,128,256]{4,3,2,1,0:T(8,128)S(1)}, f32[3,3,3,128,256]{4,3,2,1,0:T(8,128)S(1)}, u32[]{:S(2)}, u32[]{:S(2)}) collective-permute-start(f32[3,3,3,128,256]{4,3,2,1,0:T(8,128)S(1)} %fusion.53), channel_id=1, source_target_pairs={{0,64},{64,0},{128,192},{192,128},{1,65},{65,1},{129,193},{193,129... | collective-permute-start | bytes 10616840 | tf_op jit(solution)/shard_map/ppermute | solution.py:169
  419.2 88.7 %collective-permute-start.2 = (f32[3,3,3,128,256]{4,3,2,1,0:T(8,128)S(1)}, f32[3,3,3,128,256]{4,3,2,1,0:T(8,128)S(1)}, u32[]{:S(2)}, u32[]{:S(2)}) collective-permute-start(f32[3,3,3,128,256]{4,3,2,1,0:T(8,128)S(1)} %add.153), channel_id=1, source_target_pairs={{0,128},{64,192},{128,0},{192,64},{1,129},{65,193},{129,1},{193,65... | collective-permute-start | bytes 10616840 | tf_op jit(solution)/shard_map/ppermute | solution.py:169
  516.4 0.7 copy-start.11
  516.5 5.3 copy-start.3
Sparse Core Ops, SparseCore 0:
  516.6 192.7 all-reduce.8
